TPU v7x, 32 devices: a whole 2x2x4 slice. The times are simulated.
32 devices in a mesh: parts: 2 (over y), dp: 4 (over z), section: 2 (over x), chan: 2 (over core).
Axes of the slice: x: 2, y: 2, z: 4, core: 2. Of those that a mesh axis runs over, the one named last changes fastest.
Arguments:
- block_inputs: bfloat16 [2, 16, 8, 8, 1024], P('section', ('parts', 'dp')), parts along dimension 1, may hold values from -6 to 6
- out_pre: bfloat16 [2, 16, 8, 8, 1024], P('section', ('parts', 'dp')), parts along dimension 1, may hold values from -6 to 6
- first_pre: bfloat16 [2, 16, 8, 8, 1024], P('section', ('parts', 'dp'), None, None, 'chan'), parts along dimension 1, may hold values from -6 to 6
- second_pre: bfloat16 [2, 16, 8, 8, 1024], P('section', ('parts', 'dp'), None, None, 'chan'), parts along dimension 1, may hold values from -6 to 6
- w_reduce: bfloat16 [2, 1024, 1024], P('section', None, 'chan'), may hold values from -0.1875 to 0.1875
- w_group: bfloat16 [2, 9, 64, 16, 16], P('section', None, 'chan'), may hold values from -0.5 to 0.5
- w_expand: bfloat16 [2, 1024, 1024], P('section', 'chan'), may hold values from -0.1875 to 0.1875
- w_lateral: bfloat16 [1024, 256], replicated, may hold values from -0.1875 to 0.1875
- teacher: bfloat16 [16, 8, 8, 256], P(('parts', 'dp')), parts along dimension 0, may hold values from -6 to 6
- top_grad: bfloat16 [16, 8, 8, 1024], P(('parts', 'dp')), parts along dimension 0, may hold values from -6 to 6
- boxes: int32 [16, 8, 4], P(('parts', 'dp')), parts along dimension 0, may hold values from 0 to 8, as said below
- region_counts: int32 [16], P(('parts', 'dp')), parts along dimension 0, may hold values from 1 to 8
Outputs:
- input_grads: bfloat16 [2, 16, 8, 8, 1024], P('section', ('parts', 'dp')), parts along dimension 1
- reduce_grads: float32 [4, 1024, 1024], P(('parts', 'section'), 'dp', 'chan'), parts along dimension 0
- group_grads: float32 [4, 9, 64, 16, 16], P(('parts', 'section'), None, 'chan', 'dp'), parts along dimension 0
- expand_grads: float32 [4, 1024, 1024], P(('parts', 'section'), 'chan', 'dp'), parts along dimension 0
There are 2 independent parts, one for each index of `parts`. A program takes and returns all parts, laid end to end along the dimension named above; an argument that names none is the same for every part. Nothing has to cross between parts.
Inputs may be any that keep to these rules, and one draw needn't show every extreme that they name: `boxes`: each used row is a region with top < bottom and left < right; only the first region_counts[i] rows of page i are used, the others are padding.
All inputs are finite; a program needn't handle non-finite values.
Results may differ from a plain program's by a relative error of at most 0.0059.
Values may be sent and summed in bfloat16 or wider, within the bound.
A program may use at most 128 MiB of HBM per device.

v0:
```python
import math

import jax
import jax.numpy as jnp
from jax import lax
from jax.sharding import PartitionSpec as P

imitation_weight = 0.5
tap_offsets = [(tap_index // 3 - 1, tap_index % 3 - 1) for tap_index in range(9)]


def from_behind(value, axis, steps):
    count = lax.axis_size(axis)
    first, last = (max(0, -steps), min(count, count - steps))
    return lax.ppermute(value, axis, [(source, source + steps) for source in range(first, last)])


def region_mask(boxes, region_counts, crop_side):
    cells = jnp.arange(crop_side, dtype=jnp.int32)
    row_inside = (cells[None, None, :] >= boxes[:, :, 0:1]) & (
        cells[None, None, :] < boxes[:, :, 1:2]
    )
    col_inside = (cells[None, None, :] >= boxes[:, :, 2:3]) & (
        cells[None, None, :] < boxes[:, :, 3:4]
    )
    used = jnp.arange(boxes.shape[1], dtype=jnp.int32)[None, :] < region_counts[:, None]
    inside = row_inside[:, :, :, None] & col_inside[:, :, None, :] & used[:, :, None, None]
    return jnp.any(inside, axis=1).astype(jnp.float32)


def shift_stack(grid, direction, block_count, block_width):
    crop_side = grid.shape[1]
    padded = jnp.pad(grid, ((0, 0), (1, 1), (1, 1), (0, 0)))
    pieces = []
    for row_shift, col_shift in tap_offsets:
        row_start = 1 + direction * row_shift
        col_start = 1 + direction * col_shift
        pieces.append(
            padded[:, row_start : row_start + crop_side, col_start : col_start + crop_side]
        )
    return jnp.stack(pieces).reshape(9, -1, block_count, block_width)


def on_device(
    block_inputs,
    out_pre,
    first_pre,
    second_pre,
    w_reduce,
    w_group,
    w_expand,
    w_lateral,
    teacher,
    top_grad,
    boxes,
    region_counts,
):
    section_count = lax.axis_size("section")
    section_index = lax.axis_index("section")
    crop_count, crop_side = (top_grad.shape[0], top_grad.shape[1])
    channels = top_grad.shape[3]
    local_width = first_pre.shape[4]
    lateral_width = w_lateral.shape[1]
    local_groups, group_width = (w_group.shape[2], w_group.shape[3])
    block_width = min(128, local_width)
    block_count = local_width // block_width
    groups_per_block = block_width // group_width
    pixels = crop_count * crop_side * crop_side * lax.axis_size("dp")
    crop_cells = crop_side * crop_side
    page_mask = region_mask(boxes, region_counts, crop_side).reshape(-1, 1)
    covered = lax.psum(jnp.sum(page_mask), "dp")
    feature = jnp.maximum(out_pre[0], 0).reshape(-1, channels)
    lateral = jnp.dot(feature, w_lateral, preferred_element_type=jnp.float32)
    error = (
        page_mask
        * (lateral - teacher.reshape(-1, lateral_width).astype(jnp.float32))
        * (imitation_weight * pixels / covered)
    ).astype(jnp.bfloat16)
    imitation = jnp.einsum("pl,cl->pc", error, w_lateral, preferred_element_type=jnp.float32)
    start_grad = (top_grad.reshape(-1, channels).astype(jnp.float32) + imitation).astype(
        jnp.bfloat16
    )
    start_grad = start_grad.reshape(crop_count, crop_side, crop_side, channels)
    grouped = w_group[0].reshape(9, block_count, groups_per_block, group_width, group_width)
    same_group = jnp.eye(groups_per_block, dtype=bool)[None, None, :, None, :, None]
    dense_taps = jnp.where(same_group, grouped[:, :, :, :, None, :], jnp.zeros((), jnp.bfloat16))
    dense_taps = dense_taps.reshape(9, block_count, block_width, block_width)
    slab_steps = crop_count // crop_count
    round_count = section_count + slab_steps - 1
    pixel_rows = crop_count * crop_cells

    def work(crop_start, incoming):

        def take(values):
            return values[0]

        out_rows = take(out_pre).reshape(-1, channels)
        first_grid = take(first_pre)
        second_rows = take(second_pre).reshape(-1, local_width)
        passed = jnp.where(
            out_rows > 0, incoming.reshape(-1, channels), jnp.zeros((), jnp.bfloat16)
        )
        second_full = jnp.einsum(
            "pc,dc->pd", passed, w_expand[0], preferred_element_type=jnp.float32
        )
        d_second = jnp.where(second_rows > 0, second_full, jnp.zeros_like(second_full)).astype(
            jnp.bfloat16
        )
        second_grid = d_second.reshape(crop_count, crop_side, crop_side, local_width)
        second_stack = shift_stack(second_grid, -1, block_count, block_width)
        first_full = jnp.einsum(
            "tpkd,tkcd->pkc", second_stack, dense_taps, preferred_element_type=jnp.float32
        )
        first_full = first_full.reshape(-1, local_width)
        first_rows = first_grid.reshape(-1, local_width)
        d_first = jnp.where(first_rows > 0, first_full, jnp.zeros_like(first_full)).astype(
            jnp.bfloat16
        )
        return (d_first, passed, d_second)

    def spare(crop_start, incoming):
        return (
            jnp.zeros((pixel_rows, local_width), jnp.bfloat16),
            jnp.zeros((pixel_rows, channels), jnp.bfloat16),
            jnp.zeros((pixel_rows, local_width), jnp.bfloat16),
        )

    received = jnp.zeros((crop_count, crop_side, crop_side, channels), jnp.bfloat16)
    result_grads = jnp.zeros((crop_count, crop_side, crop_side, channels), jnp.bfloat16)
    passed_saved = jnp.zeros((crop_count * crop_cells, channels), jnp.bfloat16)
    second_saved = jnp.zeros((crop_count * crop_cells, local_width), jnp.bfloat16)
    first_saved = jnp.zeros((crop_count * crop_cells, local_width), jnp.bfloat16)
    for round_index in range(round_count):
        slab_index = round_index - (section_count - 1 - section_index)
        active = (slab_index >= 0) & (slab_index < slab_steps)
        crop_start = jnp.clip(slab_index, 0, slab_steps - 1) * crop_count
        incoming = jnp.where(section_index == section_count - 1, start_grad, received)
        d_first, passed, d_second = lax.cond(active, work, spare, crop_start, incoming)
        passed_saved = jnp.where(active, passed, passed_saved)
        second_saved = jnp.where(active, d_second, second_saved)
        first_saved = jnp.where(active, d_first, first_saved)
        partial_sum = lax.cond(
            active,
            lambda values: jnp.einsum(
                "pc,dc->pd", values, w_reduce[0], preferred_element_type=jnp.float32
            ),
            lambda values: jnp.zeros((pixel_rows, channels), jnp.float32),
            d_first,
        )
        share = lax.psum_scatter(partial_sum, "chan", scatter_dimension=1, tiled=True)
        share_width = channels // lax.axis_size("chan")
        own_passed = lax.dynamic_slice_in_dim(
            passed, lax.axis_index("chan") * share_width, share_width, 1
        )
        rounded = (share + own_passed.astype(jnp.float32)).astype(jnp.bfloat16)
        new_grad = lax.all_gather(rounded, "chan", axis=1, tiled=True)
        new_grad = new_grad.reshape(crop_count, crop_side, crop_side, channels)
        result_grads = jnp.where(active, new_grad, result_grads)
        if round_index + 1 < round_count:
            received = from_behind(new_grad, "section", -1)
    second_relu = jnp.maximum(second_pre[0], 0).reshape(-1, local_width)
    expand_sum = jnp.einsum(
        "pc,pd->cd", second_relu, passed_saved, preferred_element_type=jnp.float32
    )
    first_stack = shift_stack(jnp.maximum(first_pre[0], 0), 1, block_count, block_width)
    second_blocks = second_saved.reshape(-1, block_count, block_width)
    dense_grad = jnp.einsum(
        "tpkc,pkd->tkcd", first_stack, second_blocks, preferred_element_type=jnp.float32
    )
    dense_grad = dense_grad.reshape(
        9, block_count, groups_per_block, group_width, groups_per_block, group_width
    )
    group_sum = jnp.diagonal(dense_grad, axis1=2, axis2=4).transpose(0, 1, 4, 2, 3)
    group_sum = group_sum.reshape(9, local_groups, group_width, group_width)
    input_rows = block_inputs[0].reshape(-1, channels)
    reduce_sum = jnp.einsum(
        "pc,pd->cd", input_rows, first_saved, preferred_element_type=jnp.float32
    )
    reduce_part, group_part, expand_part = (
        lax.psum_scatter(reduce_sum[None], "dp", scatter_dimension=1, tiled=True),
        lax.psum_scatter(group_sum[None], "dp", scatter_dimension=3, tiled=True),
        lax.psum_scatter(expand_sum[None], "dp", scatter_dimension=2, tiled=True),
    )
    scale = 1.0 / math.sqrt(pixels)
    return (result_grads[None], reduce_part * scale, group_part * scale, expand_part * scale)


def solution(mesh):
    return jax.shard_map(
        on_device,
        mesh=mesh,
        in_specs=(
            P("section", ("parts", "dp"), None, None, None),
            P("section", ("parts", "dp"), None, None, None),
            P("section", ("parts", "dp"), None, None, "chan"),
            P("section", ("parts", "dp"), None, None, "chan"),
            P("section", None, "chan"),
            P("section", None, "chan", None, None),
            P("section", "chan", None),
            P(),
            P(("parts", "dp"), None, None, None),
            P(("parts", "dp"), None, None, None),
            P(("parts", "dp"), None, None),
            P(("parts", "dp")),
        ),
        out_specs=(
            P("section", ("parts", "dp"), None, None, None),
            P(("parts", "section"), "dp", "chan"),
            P(("parts", "section"), None, "chan", "dp", None),
            P(("parts", "section"), "chan", "dp"),
        ),
        check_vma=False,
    )
```

profile of v0, /device:TPU:0, one launch (start us, length us, event | category | flops | bytes accessed | tf_op | source)
XLA Modules:
  0.0 300.3 jit_solution(247100711332228460)
XLA Ops:
  9.7 14.1 %psum.7 = f32[]{:T(128)} all-reduce(f32[]{:T(128)} %convert_reduce_fusion), channel_id=1, replica_groups=mesh['parts'=2,'dp'=4,'section'=2,'chan'=2] {'dp'}, use_global_device_ids=true, to_apply=%region_2.0 | all-reduce | flops 1 | bytes 8 | tf_op jit(solution)/shard_map/psum | solution.py:71
  24.8 1.8 copy.117
  26.9 6.3 %broadcast_in_dim.56 = bf16[9,4,8,16,8,16]{5,4,3,2,0,1:T(8,128)(2,1)} broadcast(bf16[9,4,8,16,16]{4,3,2,0,1:T(8,128)(2,1)S(1)} %copy.118), dimensions={0,1,2,3,5} | broadcast | bytes 1327104 | tf_op jit(solution)/shard_map/jit(_where)/broadcast_in_dim | solution.py:86
  33.2 10.4 %broadcast_in_dim.57 = bf16[9,4,128,128]{3,2,0,1:T(8,128)(2,1)S(1)} reshape(bf16[9,4,8,16,8,16]{5,4,3,2,0,1:T(8,128)(2,1)} %broadcast_in_dim.56) | data formatting | bytes 2359296 | tf_op jit(solution)/shard_map/jit(_where)/broadcast_in_dim | solution.py:86
  44.7 1.6 fusion.8
  49.1 1.6 stack.90
  53.9 1.6 stack.92
  55.5 1.6 stack.93
  57.8 1.6 stack.95
  61.0 1.6 copy_dynamic-update-slice_fusion.25
  64.2 1.6 copy_dynamic-update-slice_fusion.23
  70.3 7.1 %reduce-scatter.6.cloned.1.call-done = f32[128,512]{1,0:T(8,128)} async-done(((f32[128,1024]{1,0:T(8,128)}), f32[128,512]{1,0:T(8,128)}) %reduce-scatter.6.cloned.1.call-update) | async-done | bytes 262160 | tf_op jit(solution)/shard_map/reduce_scatter | solution.py:150
  78.4 2.0 all_gather.6
  81.7 1.6 stack.98
  83.3 1.6 copy_dynamic-update-slice_fusion.18
  84.9 20.9 %collective-permute-done = bf16[2,8,8,1024]{3,2,1,0:T(8,128)(2,1)} collective-permute-done((bf16[2,8,8,1024]{3,2,1,0:T(8,128)(2,1)S(1)}, bf16[2,8,8,1024]{3,2,1,0:T(8,128)(2,1)}, u32[]{:S(2)}, u32[]{:S(2)}) %collective-permute-start) | collective-permute-done | bytes 262176 | tf_op jit(solution)/shard_map/ppermute | solution.py:15
  105.9 15.0 %conditional.6 = (bf16[128,512]{1,0:T(8,128)(2,1)}, bf16[128,1024]{1,0:T(8,128)(2,1)S(1)}, bf16[128,512]{1,0:T(8,128)(2,1)S(1)}) conditional(s32[]{:T(128)} %convert_element_type.67, () %tuple.37, (bf16[1,2,8,8,512]{4,3,2,1,0:T(8,128)(2,1)S(1)}, bf16[1,2,8,8,512]{4,3,2,1,0:T(8,128)(2,1)}, bf16[1,2,8,8,1024]{4,3,2,1,0:T(8,128)(2,1)S(1)}, pred[]{:T(512)}, ...), branch_computations={%region_8.9_spmd, %region_9.10_spmd} | conditional | flops 286064640 | bytes 15859877 | solution.py:138
  105.9 1.8 bitcast_select_fusion.3
  121.1 1.7 convolution_bitcast_fusion
  122.8 9.8 %reshape.215 = f32[9,4,8,16,8,16]{3,2,5,4,0,1:T(8,128)} reshape(f32[9,4,128,128]{2,3,0,1:T(8,128)S(1)} %convolution_bitcast_fusion) | data formatting | bytes 4718592 | tf_op jit(solution)/shard_map/reshape | solution.py:170
  132.5 18.7 %copy.129 = f32[9,4,8,16,8,16]{5,3,4,2,1,0:T(8,128)} copy(f32[9,4,8,16,8,16]{3,2,5,4,0,1:T(8,128)} %reshape.215) | data formatting | bytes 4718592 | tf_op jit(solution)/shard_map/reshape | solution.py:170
  151.2 7.1 %gather_fusion = f32[8,9,4,16,16]{4,3,2,1,0:T(8,128)S(1)} fusion(f32[9,4,16,16,8,8]{3,2,5,4,1,0:T(8,128)} %bitcast.156, s32[8]{0:T(128)S(1)} %or_bitcast_fusion), kind=kCustom, calls=%fused_computation | custom fusion | bytes 589888 | tf_op jit(solution)/shard_map/jit(diagonal)/gather | solution.py:173
  158.3 1.7 copy.130
  160.1 2.9 copy.131
  166.5 2.7 convolution_bitcast_fusion.2
  170.2 1.8 convolution_bitcast_fusion.1
  172.0 17.6 %reduce-scatter.12.cloned.1.call-done = f32[1,9,32,4,16]{2,4,1,0,3:T(8,128)} async-done(((f32[1,9,32,16,16]{2,4,1,0,3:T(8,128)}), f32[1,9,32,4,16]{2,4,1,0,3:T(8,128)}) %reduce-scatter.12.cloned.1.call-update) | async-done | bytes 73744 | tf_op jit(solution)/shard_map/reduce_scatter | solution.py:181
  191.3 7.9 %reduce-scatter.8.cloned.1.call-done = f32[128,512]{1,0:T(8,128)} async-done(((f32[128,1024]{1,0:T(8,128)}), f32[128,512]{1,0:T(8,128)}) %reduce-scatter.8.cloned.1.call-update) | async-done | bytes 262160 | tf_op jit(solution)/shard_map/reduce_scatter | solution.py:150
  200.2 2.0 all_gather.7
  202.9 43.5 %reduce-scatter.10.cloned.1.call-done = f32[1,256,512]{1,2,0:T(8,128)} async-done(((f32[1,1024,512]{1,2,0:T(8,128)}), f32[1,256,512]{1,2,0:T(8,128)}) %reduce-scatter.10.cloned.1.call-update) | async-done | bytes 524304 | tf_op jit(solution)/shard_map/reduce_scatter | solution.py:180
  248.5 43.3 %reduce-scatter.14.cloned.1.call-done = f32[1,512,256]{2,1,0:T(8,128)} async-done(((f32[1,512,1024]{2,1,0:T(8,128)}), f32[1,512,256]{2,1,0:T(8,128)}) %reduce-scatter.14.cloned.1.call-update) | async-done | bytes 524304 | tf_op jit(solution)/shard_map/reduce_scatter | solution.py:182
  291.9 1.9 broadcast_multiply_fusion
  (120 shorter events, 47.0 us)
Async XLA Ops:
  7.2 37.6 %copy-start = (bf16[1024,256]{1,0:T(8,128)(2,1)S(1)}, bf16[1024,256]{1,0:T(8,128)(2,1)}, u32[]{:S(2)}) copy-start(bf16[1024,256]{1,0:T(8,128)(2,1)} %param.27) | copy-start | bytes 1572868
  7.2 70.3 %reduce-scatter.6.cloned.1.call-start = ((), (), s32[]{:S(2)}) async-start(), calls=%async_computation.5 | async-start | bytes 786432 | tf_op jit(solution)/shard_map/reduce_scatter | solution.py:150
  44.7 1.7 copy-start.2
  44.7 1.7 copy-start.4
  47.1 1.0 copy-start.12
  48.0 141.5 %reduce-scatter.12.cloned.1.call-start = ((), (), s32[]{:S(2)}) async-start(), calls=%async_computation.8 | async-start | bytes 1474560 | tf_op jit(solution)/shard_map/reduce_scatter | solution.py:181
  49.1 11.9 %copy-start.21 = (bf16[2,8,8,512]{3,2,1,0:T(8,128)(2,1)S(1)}, bf16[2,8,8,512]{3,2,1,0:T(8,128)(2,1)}, u32[]{:S(2)}) copy-start(bf16[2,8,8,512]{3,2,1,0:T(8,128)(2,1)} %get-tuple-element.127) | copy-start | bytes 393220
  61.0 8.0 %copy-start.22 = (bf16[1,128,4,128]{3,2,1,0:T(4,128)(2,1)S(1)}, bf16[1,128,4,128]{3,2,1,0:T(4,128)(2,1)}, u32[]{:S(2)}) copy-start(bf16[1,128,4,128]{3,2,1,0:T(4,128)(2,1)} %stack.96) | copy-start | bytes 393220
  80.4 25.5 %copy-start.17 = (bf16[128,1024]{1,0:T(8,128)(2,1)}, bf16[128,1024]{1,0:T(8,128)(2,1)S(1)}, u32[]{:S(2)}) copy-start(bf16[128,1024]{1,0:T(8,128)(2,1)S(1)} %all_gather.6) | copy-start | bytes 786436
  80.4 25.4 %collective-permute-start = (bf16[2,8,8,1024]{3,2,1,0:T(8,128)(2,1)S(1)}, bf16[2,8,8,1024]{3,2,1,0:T(8,128)(2,1)}, u32[]{:S(2)}, u32[]{:S(2)}) collective-permute-start(bf16[2,8,8,1024]{3,2,1,0:T(8,128)(2,1)S(1)} %bitcast.165), channel_id=1, source_target_pairs={{2,0},{3,1},{6,4},{7,5},{10,8},{11,9},{14,12},{15,13},{18,16},{19,... | collective-permute-start | bytes 786440 | tf_op jit(solution)/shard_map/ppermute | solution.py:15
  105.9 1.8 copy-start.16
  108.9 9.1 %copy-start.7 = (bf16[128,512]{1,0:T(8,128)(2,1)}, bf16[128,512]{1,0:T(8,128)(2,1)S(1)}, u32[]{:S(2)}) copy-start(bf16[128,512]{1,0:T(8,128)(2,1)S(1)} %fusion.4) | copy-start | bytes 393220 | tf_op jit(solution)/shard_map/cond
  118.4 0.8 copy-start.25
  118.4 1.5 copy-start.20
  118.9 1.9 copy-start.8
  120.9 1.9 copy-start.10
  162.9 1.2 copy-start.3
  163.0 36.2 %reduce-scatter.8.cloned.1.call-start = ((), (), s32[]{:S(2)}) async-start(), calls=%async_computation.6 | async-start | bytes 786432 | tf_op jit(solution)/shard_map/reduce_scatter | solution.py:150
  164.2 2.3 copy-start.23
  165.6 0.8 copy-start.9
  166.4 80.0 %reduce-scatter.10.cloned.1.call-start = ((), (), s32[]{:S(2)}) async-start(), calls=%async_computation.7 | async-start | bytes 2621440 | tf_op jit(solution)/shard_map/reduce_scatter | solution.py:180
  169.2 0.9 copy-start.14
  169.2 1.0 copy-start.11
  169.2 122.7 %reduce-scatter.14.cloned.1.call-start = ((), (), s32[]{:S(2)}) async-start(), calls=%async_computation.9 | async-start | bytes 2621440 | tf_op jit(solution)/shard_map/reduce_scatter | solution.py:182
  172.0 30.1 %copy-start.18 = (bf16[128,1024]{1,0:T(8,128)(2,1)S(1)}, bf16[128,1024]{1,0:T(8,128)(2,1)}, u32[]{:S(2)}) copy-start(bf16[128,1024]{1,0:T(8,128)(2,1)} %copy-done.17) | copy-start | bytes 786436
  246.4 47.4 %copy-start.1 = (bf16[1024,256]{1,0:T(8,128)(2,1)S(1)}, bf16[1024,256]{1,0:T(8,128)(2,1)}, u32[]{:S(2)}) copy-start(bf16[1024,256]{1,0:T(8,128)(2,1)} %param.27) | copy-start | bytes 1572868
Sparse Core Ops, SparseCore 0:
  48.2 29.2 reduce-scatter.5
  163.1 26.4 reduce-scatter.11
  192.5 6.6 reduce-scatter.7
  201.3 45.0 reduce-scatter.9
  248.6 43.1 reduce-scatter.13
where the time goes:
time: 302 us; the launch traced here: 300 us
  waiting for transfers between devices  140 us (46%)
  local copies, waits for them, and re-layouts  102 us (34%)
  blocking collectives  18.1 us (6%)
  between operations  14.8 us (5%)
  other arithmetic  13.5 us (4%)
  matrix products  10.3 us (3%)
    reduce_scatter x1, waiting for transfers between devices, on_device(): lax.psum_scatter(reduce_sum[None], 'dp', scatter_dimension=1, tiled=True)  43.5 us
    reduce_scatter x1, waiting for transfers between devices, on_device(): lax.psum_scatter(expand_sum[None], 'dp', scatter_dimension=2, tiled=True)  43.3 us
    reshape x2, local copies, waits for them, and re-layouts, on_device(): dense_grad.reshape(9, block_count, groups_per_block, group_width, groups_...  28.4 us
    ppermute x1, waiting for transfers between devices, from_behind(): lax.ppermute(value, axis, [(source, source + steps) for source in range(f...  20.9 us
    another operation x20, local copies, waits for them, and re-layouts, shift_stack(): return jnp.stack(pieces).reshape(9, -1, block_count, block_width)  18.3 us
    reduce_scatter x1, waiting for transfers between devices, on_device(): lax.psum_scatter(group_sum[None], 'dp', scatter_dimension=3, tiled=True)  17.6 us
    unnamed x41, local copies, waits for them, and re-layouts  17.4 us
    broadcast_in_dim x5, local copies, waits for them, and re-layouts, on_device(): jnp.where(same_group, grouped[:, :, :, :, None, :], jnp.zeros((), jnp.bfl...  17.3 us
  transfers between devices with their start and end apart: 6, of which 6 were waited for; matrix products, arithmetic and copies ran while one was open for 12% of the time, Pallas kernels for 0%

commit v1 on v0

v1 whole, which is shorter than its diff:
```python
import functools
import math

import jax
import jax.numpy as jnp
from jax import lax
from jax.experimental import pallas as pl
from jax.experimental.pallas import tpu as pltpu
from jax.sharding import PartitionSpec as P

imitation_weight = 0.5
tap_offsets = [(tap // 3 - 1, tap % 3 - 1) for tap in range(9)]
f32 = jnp.float32
bf16 = jnp.bfloat16


def dot_nn(a, b):
    return lax.dot_general(a, b, (((1,), (0,)), ((), ())), preferred_element_type=f32)


def dot_nt(a, b):
    return lax.dot_general(a, b, (((1,), (1,)), ((), ())), preferred_element_type=f32)


def dot_tn(a, b):
    return lax.dot_general(a, b, (((0,), (0,)), ((), ())), preferred_element_type=f32)


def kernel(
    dims,
    boxes_ref, counts_ref, bi_ref, out_ref, first_ref, second_ref, wr_ref, wg_ref, we_ref,
    wl_ref, teacher_ref, top_ref,
    grads_ref, reduce_ref, group_ref, expand_ref,
    inc, pas, wr_peer, dfx, ng, d_all, sec_all, bi_send, bi_all, ps_send, ps_all,
    gf, g_send, g_all, cnt, taps, ft,
    dp_send, dp_recv, core_send, core_recv, hop_send, hop_recv, fwd_send, fwd_recv,
):
    n, sections, crops, side, slots, pixels = dims
    rows, channels = bi_ref.shape
    half = channels // 2
    width = first_ref.shape[1]
    gw = wg_ref.shape[1]
    blk = taps.shape[2]
    blocks = width // blk
    cells = side * side
    share = channels // n
    k = gw // n
    hrows = rows // 2
    me = lax.axis_index("dp")
    s = lax.axis_index("section")
    c = lax.axis_index("chan")
    other = 1 - c
    last = sections - 1

    def remote(src, dst, send, recv, where):
        return pltpu.make_async_remote_copy(
            src_ref=src, dst_ref=dst, send_sem=send, recv_sem=recv,
            device_id=where, device_id_type=pl.DeviceIdType.MESH,
        )

    def dp_copies(what, src_of, dst):
        out = []
        for step in range(1, n):
            to = lax.rem(me + step, n)
            out.append(remote(src_of(to), dst, dp_send.at[what, step - 1],
                              dp_recv.at[what, step - 1], {"dp": to}))
        return out

    barrier = pltpu.get_barrier_semaphore()
    mesh_type = pl.DeviceIdType.MESH
    for step in range(1, n):
        pl.semaphore_signal(barrier, inc=1, device_id={"dp": lax.rem(me + step, n)},
                            device_id_type=mesh_type)
    pl.semaphore_signal(barrier, inc=1, device_id={"chan": other}, device_id_type=mesh_type)

    @pl.when(s > 0)
    def _():
        pl.semaphore_signal(barrier, inc=1, device_id={"section": s - 1},
                            device_id_type=mesh_type)

    @pl.when(s < last)
    def _():
        pl.semaphore_signal(barrier, inc=1, device_id={"section": s + 1},
                            device_id_type=mesh_type)

    row = lax.broadcasted_iota(jnp.int32, (cells, 128), 0)
    row_h, row_w = row // side, row % side
    masks = []
    for crop in range(crops):
        inside = jnp.zeros((cells, 128), f32)
        for r in range(slots):
            hit = ((row_h >= boxes_ref[crop, 4 * r]) & (row_h < boxes_ref[crop, 4 * r + 1])
                   & (row_w >= boxes_ref[crop, 4 * r + 2]) & (row_w < boxes_ref[crop, 4 * r + 3])
                   & (counts_ref[0, crop] > r))
            inside = jnp.where(hit, 1.0, inside)
        masks.append(inside)
    mask = jnp.concatenate(masks, axis=0)
    cnt[me] = jnp.broadcast_to(jnp.sum(mask, axis=0, keepdims=True), (8, 128))
    sec_all[me] = jnp.maximum(second_ref[...], 0)
    for j in range(n):
        bi_send[j] = bi_ref[:, j * share : (j + 1) * share]
    bi_all[me] = bi_send[me]

    pl.semaphore_wait(barrier, n + jnp.where(s > 0, 1, 0) + jnp.where(s < last, 1, 0))

    cnt_copies = dp_copies(0, lambda to: cnt.at[me], cnt.at[me])
    wr_copy = remote(wr_ref.at[pl.ds(pl.multiple_of(other * half, half), half)], wr_peer,
                     core_send.at[0], core_recv.at[0], {"chan": other})
    sec_copies = dp_copies(1, lambda to: sec_all.at[me], sec_all.at[me])
    bi_copies = dp_copies(2, lambda to: bi_send.at[to], bi_all.at[me])
    for copy in cnt_copies + [wr_copy] + sec_copies + bi_copies:
        copy.start()

    sel = (lax.broadcasted_iota(jnp.int32, (gw, blk), 1) % gw
           == lax.broadcasted_iota(jnp.int32, (gw, blk), 0)).astype(f32).astype(bf16)
    same = (lax.broadcasted_iota(jnp.int32, (blk, blk), 0) // gw
            == lax.broadcasted_iota(jnp.int32, (blk, blk), 1) // gw)
    for t in range(9):
        for b in range(blocks):
            base = t * width + b * blk
            dense = dot_nn(wg_ref[base : base + blk, :], sel)
            taps[t, b * blk : (b + 1) * blk, :] = jnp.where(same, dense, 0.0).astype(bf16)

    prow = lax.broadcasted_iota(jnp.int32, (rows, blk), 0)
    p_w = prow % side
    p_h = (prow // side) % side

    def h_ok(a):
        return p_h >= 1 if a == 1 else p_h < side - 1

    def w_ok(b):
        return p_w >= 1 if b == 1 else p_w < side - 1

    def moved(x, a, b):
        shift = (side * a + b) % rows
        if shift:
            x = pltpu.roll(x, shift, 0)
        if a:
            x = jnp.where(h_ok(a), x, 0.0)
        if b:
            x = jnp.where(w_ok(b), x, 0.0)
        return x

    def prepare_first():
        for b in range(blocks):
            first = jnp.maximum(first_ref[:, b * blk : (b + 1) * blk], 0).astype(f32)
            for t, (da, db) in enumerate(tap_offsets):
                ft[t, b] = moved(first, -da, -db).T.astype(bf16)

    hop_copies = [
        remote(ng.at[c, pl.ds(q * hrows, hrows)], inc.at[c, pl.ds(q * hrows, hrows)],
               hop_send.at[q], hop_recv.at[q], {"section": lax.max(s - 1, 0)})
        for q in range(2)
    ]
    fwd_copies = [
        remote(inc.at[c, pl.ds(q * hrows, hrows)], inc.at[c, pl.ds(q * hrows, hrows)],
               fwd_send.at[q], fwd_recv.at[q], {"chan": other})
        for q in range(2)
    ]

    @pl.when(s == last)
    def _():
        feature = jnp.maximum(out_ref[...], 0)
        lateral = dot_nn(feature, wl_ref[...])
        error = (mask[:, 0:1] * (lateral - teacher_ref[...].astype(f32))).astype(bf16)
        imitation = dot_nt(error, wl_ref[...])
        for copy in cnt_copies:
            copy.wait_recv()
        covered = cnt[0]
        for j in range(1, n):
            covered = covered + cnt[j]
        scale = (imitation_weight * pixels) / covered[0:1, 0:1]
        start = (top_ref[...].astype(f32) + imitation * scale).astype(bf16)
        start = jnp.where(out_ref[...] > 0, start, jnp.zeros_like(start))
        pas[0] = start[:, :half]
        pas[1] = start[:, half:]

    @pl.when(s < last)
    def _():
        for copy in cnt_copies:
            copy.wait_recv()
        prepare_first()
        for q in range(2):
            hop_copies[q].wait_recv()
            fwd_copies[q].start()
        for q in range(2):
            fwd_copies[q].wait_recv()
        for q in range(2):
            value = inc[q]
            gate = out_ref[:, q * half : (q + 1) * half] > 0
            pas[q] = jnp.where(gate, value, jnp.zeros_like(value))

    for j in range(n):
        lo = j * share
        q = lo // half
        ps_send[j] = pas[q, :, lo - q * half : lo - q * half + share]
    ps_all[me] = ps_send[me]
    ps_copies = dp_copies(3, lambda to: ps_send.at[to], ps_all.at[me])
    for copy in ps_copies:
        copy.start()

    second_full = dot_nt(pas[0], we_ref[:, :half]) + dot_nt(pas[1], we_ref[:, half:])
    d_second = jnp.where(second_ref[...] > 0, second_full, 0.0).astype(bf16)
    pieces = []
    for b in range(blocks):
        lhs = d_second[:, b * blk : (b + 1) * blk]
        total = None
        for db in (-1, 0, 1):
            column = None
            for da in (-1, 0, 1):
                t = 3 * (da + 1) + db + 1
                y = moved(dot_nt(lhs, taps[t, b * blk : (b + 1) * blk, :]), da, 0)
                column = y if column is None else column + y
            column = moved(column, 0, db)
            total = column if total is None else total + column
        pieces.append(jnp.where(first_ref[:, b * blk : (b + 1) * blk] > 0, total, 0.0).astype(bf16))
    d_first = jnp.concatenate(pieces, axis=1)
    d_all[me] = d_first

    dfx_copy = remote(d_all.at[me], dfx, core_send.at[1], core_recv.at[1], {"chan": other})
    dfx_copy.start()
    d_copies = dp_copies(4, lambda to: d_all.at[me], d_all.at[me])
    for copy in d_copies:
        copy.start()

    own_rows = pl.ds(pl.multiple_of(c * half, half), half)
    grad = dot_nt(d_first, wr_ref[own_rows, :]) + pas[c].astype(f32)
    wr_copy.wait_recv()
    dfx_copy.wait_recv()
    grad = grad + dot_nt(dfx[...], wr_peer[...])
    ng[c] = grad.astype(bf16)
    ng_copy = remote(ng.at[c], ng.at[c], core_send.at[2], core_recv.at[2], {"chan": other})

    @pl.when(s > 0)
    def _():
        for copy in hop_copies:
            copy.start()

    ng_copy.start()

    @pl.when(s == last)
    def _():
        prepare_first()

    gf[...] = jnp.zeros_like(gf)
    for b in range(blocks):
        rhs = d_second[:, b * blk : (b + 1) * blk]
        for t in range(9):
            dense = jnp.where(same, dot_nn(ft[t, b], rhs), 0.0)
            folded = jnp.sum(dense.reshape(blk // gw, gw, blk), axis=0)
            for j in range(n):
                gf[j, t * k : (t + 1) * k, b * blk : (b + 1) * blk] = folded[j * k : (j + 1) * k]
    g_send[...] = gf[...].astype(bf16)
    g_copies = dp_copies(5, lambda to: g_send.at[to], g_all.at[me])
    for copy in g_copies:
        copy.start()

    norm = 1.0 / math.sqrt(pixels)
    for copy in sec_copies + ps_copies:
        copy.wait_recv()
    expand = dot_tn(sec_all[...].reshape(n * rows, width), ps_all[...].reshape(n * rows, share))
    expand_ref[...] = expand * norm
    for copy in bi_copies + d_copies:
        copy.wait_recv()
    reduced = dot_tn(bi_all[...].reshape(n * rows, share), d_all[...].reshape(n * rows, width))
    reduce_ref[...] = reduced * norm
    for copy in g_copies:
        copy.wait_recv()
    g_all[me] = jnp.zeros(g_all.shape[1:], bf16)
    total = gf[me]
    for j in range(n):
        total = total + g_all[j].astype(f32)
    group_ref[...] = total * norm
    ng_copy.wait_recv()
    grads_ref[:, :half] = ng[0]
    grads_ref[:, half:] = ng[1]

    for copy in cnt_copies + sec_copies + bi_copies + ps_copies + d_copies + g_copies:
        copy.wait_send()
    for copy in (wr_copy, dfx_copy, ng_copy):
        copy.wait_send()

    @pl.when(s > 0)
    def _():
        for copy in hop_copies:
            copy.wait_send()

    @pl.when(s < last)
    def _():
        for copy in fwd_copies:
            copy.wait_send()


def on_device(
    block_inputs, out_pre, first_pre, second_pre, w_reduce, w_group, w_expand, w_lateral,
    teacher, top_grad, boxes, region_counts,
):
    n = lax.axis_size("dp")
    sections = lax.axis_size("section")
    crops, side, _, channels = top_grad.shape
    rows = crops * side * side
    width = first_pre.shape[4]
    lateral_width = w_lateral.shape[1]
    groups, gw = w_group.shape[2], w_group.shape[3]
    slots = boxes.shape[1]
    pixels = rows * n
    share = channels // n
    k = gw // n
    grows = -(-9 * k // 16) * 16
    half = channels // 2
    blk = min(256, width)
    vmem = pl.BlockSpec(memory_space=pltpu.VMEM)
    smem = pl.BlockSpec(memory_space=pltpu.SMEM)
    dma = pltpu.SemaphoreType.DMA
    peers = max(n - 1, 1)
    grads, reduced, group, expand = pl.pallas_call(
        functools.partial(kernel, (n, sections, crops, side, slots, pixels)),
        out_shape=(
            jax.ShapeDtypeStruct((rows, channels), bf16),
            jax.ShapeDtypeStruct((share, width), f32),
            jax.ShapeDtypeStruct((grows, width), f32),
            jax.ShapeDtypeStruct((width, share), f32),
        ),
        in_specs=[smem, smem] + [vmem] * 10,
        out_specs=(vmem,) * 4,
        scratch_shapes=[
            pltpu.VMEM((2, rows, half), bf16),
            pltpu.VMEM((2, rows, half), bf16),
            pltpu.VMEM((half, width), bf16),
            pltpu.VMEM((rows, width), bf16),
            pltpu.VMEM((2, rows, half), bf16),
            pltpu.VMEM((n, rows, width), bf16),
            pltpu.VMEM((n, rows, width), bf16),
            pltpu.VMEM((n, rows, share), bf16),
            pltpu.VMEM((n, rows, share), bf16),
            pltpu.VMEM((n, rows, share), bf16),
            pltpu.VMEM((n, rows, share), bf16),
            pltpu.VMEM((n, grows, width), f32),
            pltpu.VMEM((n, grows, width), bf16),
            pltpu.VMEM((n, grows, width), bf16),
            pltpu.VMEM((n, 8, 128), f32),
            pltpu.VMEM((9, width, blk), bf16),
            pltpu.VMEM((9, width // blk, blk, rows), bf16),
            dma((6, peers)), dma((6, peers)), dma((3,)), dma((3,)),
            dma((2,)), dma((2,)), dma((2,)), dma((2,)),
        ],
        compiler_params=pltpu.CompilerParams(
            collective_id=0, has_side_effects=True, vmem_limit_bytes=56 << 20,
        ),
    )(
        boxes.reshape(crops, slots * 4), region_counts.reshape(1, crops),
        block_inputs.reshape(rows, channels), out_pre.reshape(rows, channels),
        first_pre.reshape(rows, width), second_pre.reshape(rows, width),
        w_reduce[0], w_group.reshape(9 * groups * gw, gw), w_expand[0], w_lateral,
        teacher.reshape(rows, lateral_width), top_grad.reshape(rows, channels),
    )
    group = group[: 9 * k].reshape(9, k, groups, gw).transpose(0, 2, 1, 3)
    return (
        grads.reshape(1, crops, side, side, channels), reduced[None], group[None], expand[None],
    )


def solution(mesh):
    return jax.shard_map(
        on_device,
        mesh=mesh,
        in_specs=(
            P("section", ("parts", "dp"), None, None, None),
            P("section", ("parts", "dp"), None, None, None),
            P("section", ("parts", "dp"), None, None, "chan"),
            P("section", ("parts", "dp"), None, None, "chan"),
            P("section", None, "chan"),
            P("section", None, "chan", None, None),
            P("section", "chan", None),
            P(),
            P(("parts", "dp"), None, None, None),
            P(("parts", "dp"), None, None, None),
            P(("parts", "dp"), None, None),
            P(("parts", "dp")),
        ),
        out_specs=(
            P("section", ("parts", "dp"), None, None, None),
            P(("parts", "section"), "dp", "chan"),
            P(("parts", "section"), None, "chan", "dp", None),
            P(("parts", "section"), "chan", "dp"),
        ),
        check_vma=False,
    )
```

time: 302 us -> 57 us (0.19)
  waiting for transfers between devices: 140 us -> 0 us
  local copies, waits for them, and re-layouts: 102 us -> 8.31 us
  Pallas kernels: 0 us -> 47.9 us
  blocking collectives: 18.1 us -> 0 us
  between operations: 14.8 us -> 0.68 us
  other arithmetic: 13.5 us -> 0 us
  matrix products: 10.3 us -> 0 us
    reduce_scatter x5 -> x0, waiting for transfers between devices: 119 us -> none  [the longest x1 43.5 us: on_device(): lax.psum_scatter(reduce_sum[None], 'dp', scatter_dimension=1, tiled=True)]
    pallas_call x0 -> x1, Pallas kernels: none -> 47.9 us  [on_device(): pl.pallas_call(functools.partial(kernel, (n, sections, crops, side, slots...]
    reshape x4 -> x2, local copies, waits for them, and re-layouts: 28.7 us -> 0.86 us  [the longest x1 0.64 us: on_device(): boxes.reshape(crops, slots * 4)]
    another operation x25 -> x0, local copies, waits for them, and re-layouts: 22.7 us -> none  [the longest x20 18.3 us: shift_stack(): return jnp.stack(pieces).reshape(9, -1, block_count, block_width)]
    ppermute x1 -> x0, waiting for transfers between devices: 20.9 us -> none  [from_behind(): lax.ppermute(value, axis, [(source, source + steps) for source in range(f...]
    broadcast_in_dim x5 -> x0, local copies, waits for them, and re-layouts: 17.3 us -> none  [on_device(): jnp.where(same_group, grouped[:, :, :, :, None, :], jnp.zeros((), jnp.bfl...]
    psum x1 -> x0, blocking collectives: 14.1 us -> none  [on_device(): covered = lax.psum(jnp.sum(page_mask), 'dp')]
    unnamed x41 -> x12, local copies, waits for them, and re-layouts: 17.4 us -> 6.49 us
  transfers between devices with their start and end apart: 6 -> 0, of which waited for: 6 -> 0; matrix products, arithmetic and copies ran while one was open for 12% -> 0% of each run, Pallas kernels for 0% -> 0%
where the time goes in v1:
time: 57 us; the launch traced here: 56.9 us
  Pallas kernels  47.9 us (84%)
  local copies, waits for them, and re-layouts  8.31 us (15%)
  between operations  0.68 us (1%)
    pallas_call x1, Pallas kernels, on_device(): pl.pallas_call(functools.partial(kernel, (n, sections, crops, side, slots...  47.9 us
    unnamed x12, local copies, waits for them, and re-layouts  6.49 us

profile of v1, /device:TPU:0, one launch (start us, length us, event | category | flops | bytes accessed | tf_op | source)
XLA Modules:
  0.0 56.9 jit_solution(1835587207779433748)
XLA Ops:
  0.6 0.8 %copy.19 = s32[2,8,4]{2,1,0:T(8,128)S(1)} copy(s32[2,8,4]{1,2,0:T(4,128)} %param.22) | data formatting | bytes 512 | tf_op args[10]
  1.4 0.6 %reshape.41.boxes_ref = s32[2,32]{1,0:T(2,128)} reshape(s32[2,8,4]{2,1,0:T(8,128)S(1)} %copy.19) | data formatting | bytes 512 | tf_op jit(solution)/shard_map/reshape | solution.py:351
  2.0 2.5 %copy.20 = bf16[1,9,32,16,16]{4,3,2,1,0:T(8,128)(2,1)} copy(bf16[1,9,32,16,16]{2,4,3,1,0:T(8,128)(2,1)} %param.17) | data formatting | bytes 294912 | tf_op args[5]
  4.5 47.9 %shard_map.147 = (bf16[128,1024]{1,0:T(8,128)(2,1)}, f32[256,512]{1,0:T(8,128)}, f32[48,512]{1,0:T(8,128)}, f32[512,256]{1,0:T(8,128)}) custom-call(s32[2,32]{1,0:T(2,128)} %reshape.41.boxes_ref, s32[1,2]{1,0:T(1,128)} %bitcast.29, bf16[128,1024]{1,0:T(8,128)(2,1)} %bitcast.22, bf16[128,1024]{1,0:T(8,128)(2,1)} %bitcast.23, bf16[128,512]{1,0:T(8,128)(2,1)} %bitcast.26, ...), custom_call_target="tpu_custom_call" | custom-call | tf_op jit(solution)/shard_map/pallas_call | solution.py:316
  52.4 0.0 copy-start.2
  52.4 0.0 copy-start.1
  52.4 1.0 %slice.3 = f32[36,512]{1,0:T(8,128)S(1)} slice(f32[48,512]{1,0:T(8,128)} %get-tuple-element.10), slice={[0:36], [0:512]} | slice | bytes 147456 | tf_op jit(solution)/shard_map/slice | solution.py:357
  53.4 0.2 reshape.51
  53.6 0.0 copy-start
  53.6 0.9 %copy.21 = f32[1,9,32,4,16]{2,4,3,1,0:T(8,128)} copy(f32[1,9,32,4,16]{4,2,3,1,0:T(8,128)S(1)} %bitcast.17) | data formatting | bytes 147456
  54.6 0.0 copy-done.2
  54.6 0.7 %copy.25 = bf16[1,2,8,8,1024]{4,3,2,1,0:T(8,128)(2,1)} copy(bf16[1,2,8,8,1024]{4,3,2,1,0:T(8,128)(2,1)S(1)} %bitcast.25) | data formatting | bytes 524288
  55.3 0.0 copy-done.1
  55.3 0.8 %copy.26 = f32[1,256,512]{2,1,0:T(8,128)} copy(f32[1,256,512]{2,1,0:T(8,128)S(1)} %bitcast.21) | data formatting | bytes 1048576
  56.1 0.0 copy-done
  56.1 0.8 %copy.27 = f32[1,512,256]{2,1,0:T(8,128)} copy(f32[1,512,256]{2,1,0:T(8,128)S(1)} %bitcast.20) | data formatting | bytes 1048576
Async XLA Ops:
  52.4 2.2 %copy-start.2 = (bf16[128,1024]{1,0:T(8,128)(2,1)S(1)}, bf16[128,1024]{1,0:T(8,128)(2,1)}, u32[]{:S(2)}) copy-start(bf16[128,1024]{1,0:T(8,128)(2,1)} %get-tuple-element.8) | copy-start | bytes 786436
  52.4 2.8 %copy-start.1 = (f32[256,512]{1,0:T(8,128)S(1)}, f32[256,512]{1,0:T(8,128)}, u32[]{:S(2)}) copy-start(f32[256,512]{1,0:T(8,128)} %get-tuple-element.9) | copy-start | bytes 1572868
  53.6 2.4 %copy-start = (f32[512,256]{1,0:T(8,128)S(1)}, f32[512,256]{1,0:T(8,128)}, u32[]{:S(2)}) copy-start(f32[512,256]{1,0:T(8,128)} %get-tuple-element.11) | copy-start | bytes 1572868

commit v2 on v1

--- a/solution.py
+++ b/solution.py
@@ -28,18 +28,22 @@
 
 def kernel(
     dims,
-    boxes_ref, counts_ref, bi_ref, out_ref, first_ref, second_ref, wr_ref, wg_ref, we_ref,
-    wl_ref, teacher_ref, top_ref,
-    grads_ref, reduce_ref, group_ref, expand_ref,
+    boxes_ref, counts_ref, bi_hbm, out_hbm, first_hbm, second_hbm, wr_hbm, wg_hbm, we_hbm,
+    wl_hbm, teacher_hbm, top_hbm,
+    grads_hbm, reduce_hbm, group_hbm, expand_hbm,
+    bi_ref, out_ref, first_ref, second_ref, wr_ref, wg_ref, we_ref, wl_ref, teacher_ref, top_ref,
+    reduce_ref, group_ref, expand_ref, load_sem, store_sem,
     inc, pas, wr_peer, dfx, ng, d_all, sec_all, bi_send, bi_all, ps_send, ps_all,
     gf, g_send, g_all, cnt, taps, ft,
     dp_send, dp_recv, core_send, core_recv, hop_send, hop_recv, fwd_send, fwd_recv,
+    right_send, right_recv, left_send, left_recv, share_send, share_recv,
 ):
     n, sections, crops, side, slots, pixels = dims
     rows, channels = bi_ref.shape
     half = channels // 2
     width = first_ref.shape[1]
-    gw = wg_ref.shape[1]
+    groups = wg_ref.shape[1]
+    gw = width // groups
     blk = taps.shape[2]
     blocks = width // blk
     cells = side * side
@@ -66,6 +70,35 @@
                               dp_recv.at[what, step - 1], {"dp": to}))
         return out
 
+    mine = pl.ds(pl.multiple_of(c * hrows, hrows), hrows)
+
+    def share_copies(which, buf):
+        out = []
+        for step in range(1, n):
+            rows_ref = buf.at[lax.rem(me + n - step, n), mine]
+            out.append(remote(rows_ref, rows_ref, share_send.at[which, step - 1],
+                              share_recv.at[which, step - 1], {"chan": other}))
+        return out
+
+    def line(step, buf):
+        ahead, behind = buf.at[lax.max(me - step, 0)], buf.at[lax.min(me + step, n - 1)]
+        right = remote(ahead, ahead, right_send.at[step], right_recv.at[step],
+                       {"dp": lax.min(me + 1, n - 1)})
+        left = remote(behind, behind, left_send.at[step], left_recv.at[step],
+                      {"dp": lax.max(me - 1, 0)})
+        return (
+            (right, (me - step >= 0) & (me + 1 < n), me - 1 - step >= 0),
+            (left, (me + step < n) & (me >= 1), me + 1 + step < n),
+        )
+
+    def line_start(moves):
+        for copy, sends, _ in moves:
+            pl.when(sends)(copy.start)
+
+    def line_recv(moves):
+        for copy, _, receives in moves:
+            pl.when(receives)(copy.wait_recv)
+
     barrier = pltpu.get_barrier_semaphore()
     mesh_type = pl.DeviceIdType.MESH
     for step in range(1, n):
@@ -83,19 +116,31 @@
         pl.semaphore_signal(barrier, inc=1, device_id={"section": s + 1},
                             device_id_type=mesh_type)
 
+    pairs = [
+        (second_hbm, second_ref), (bi_hbm, bi_ref), (wr_hbm, wr_ref), (out_hbm, out_ref),
+        (wl_hbm, wl_ref), (teacher_hbm, teacher_ref), (top_hbm, top_ref), (we_hbm, we_ref),
+        (wg_hbm, wg_ref), (first_hbm, first_ref),
+    ]
+    loads = [pltpu.make_async_copy(a, b, load_sem.at[i]) for i, (a, b) in enumerate(pairs)]
+    for load in loads:
+        load.start()
+
     row = lax.broadcasted_iota(jnp.int32, (cells, 128), 0)
     row_h, row_w = row // side, row % side
     masks = []
     for crop in range(crops):
         inside = jnp.zeros((cells, 128), f32)
         for r in range(slots):
-            hit = ((row_h >= boxes_ref[crop, 4 * r]) & (row_h < boxes_ref[crop, 4 * r + 1])
-                   & (row_w >= boxes_ref[crop, 4 * r + 2]) & (row_w < boxes_ref[crop, 4 * r + 3])
+            hit = ((row_h >= boxes_ref[crop, 0, r]) & (row_h < boxes_ref[crop, 1, r])
+                   & (row_w >= boxes_ref[crop, 2, r]) & (row_w < boxes_ref[crop, 3, r])
                    & (counts_ref[0, crop] > r))
             inside = jnp.where(hit, 1.0, inside)
         masks.append(inside)
     mask = jnp.concatenate(masks, axis=0)
     cnt[me] = jnp.broadcast_to(jnp.sum(mask, axis=0, keepdims=True), (8, 128))
+    loads[0].wait()
+    loads[1].wait()
+    loads[2].wait()
     sec_all[me] = jnp.maximum(second_ref[...], 0)
     for j in range(n):
         bi_send[j] = bi_ref[:, j * share : (j + 1) * share]
@@ -107,18 +152,23 @@
     wr_copy = remote(wr_ref.at[pl.ds(pl.multiple_of(other * half, half), half)], wr_peer,
                      core_send.at[0], core_recv.at[0], {"chan": other})
     sec_copies = dp_copies(1, lambda to: sec_all.at[me], sec_all.at[me])
-    bi_copies = dp_copies(2, lambda to: bi_send.at[to], bi_all.at[me])
+    bi_copies = dp_copies(2, lambda to: bi_send.at[to, mine], bi_all.at[me, mine])
     for copy in cnt_copies + [wr_copy] + sec_copies + bi_copies:
         copy.start()
 
-    sel = (lax.broadcasted_iota(jnp.int32, (gw, blk), 1) % gw
-           == lax.broadcasted_iota(jnp.int32, (gw, blk), 0)).astype(f32).astype(bf16)
-    same = (lax.broadcasted_iota(jnp.int32, (blk, blk), 0) // gw
-            == lax.broadcasted_iota(jnp.int32, (blk, blk), 1) // gw)
-    for t in range(9):
-        for b in range(blocks):
-            base = t * width + b * blk
-            dense = dot_nn(wg_ref[base : base + blk, :], sel)
+    loads[8].wait()
+    pair = gw * gw
+    iota = lambda shape, dim: lax.broadcasted_iota(jnp.int32, shape, dim)
+    same = iota((blk, blk), 0) // gw == iota((blk, blk), 1) // gw
+    same_out = iota((blk, pair), 0) % gw == iota((blk, pair), 1) % gw
+    spread = (iota((pair, blk), 0) // gw == iota((pair, blk), 1) % gw).astype(f32).astype(bf16)
+    for b in range(blocks):
+        pick = (iota((blk, groups), 1) == b * (blk // gw) + iota((blk, groups), 0) // gw)
+        pick = pick.astype(f32).astype(bf16)
+        for t in range(9):
+            values = dot_nt(pick, wg_ref[t * pair : (t + 1) * pair, :])
+            values = jnp.where(same_out, values, 0.0).astype(bf16)
+            dense = dot_nn(values, spread)
             taps[t, b * blk : (b + 1) * blk, :] = jnp.where(same, dense, 0.0).astype(bf16)
 
     prow = lax.broadcasted_iota(jnp.int32, (rows, blk), 0)
@@ -146,6 +196,9 @@
             first = jnp.maximum(first_ref[:, b * blk : (b + 1) * blk], 0).astype(f32)
             for t, (da, db) in enumerate(tap_offsets):
                 ft[t, b] = moved(first, -da, -db).T.astype(bf16)
+
+    for i in (3, 4, 5, 6, 7, 9):
+        loads[i].wait()
 
     hop_copies = [
         remote(ng.at[c, pl.ds(q * hrows, hrows)], inc.at[c, pl.ds(q * hrows, hrows)],
@@ -162,15 +215,15 @@
     def _():
         feature = jnp.maximum(out_ref[...], 0)
         lateral = dot_nn(feature, wl_ref[...])
-        error = (mask[:, 0:1] * (lateral - teacher_ref[...].astype(f32))).astype(bf16)
-        imitation = dot_nt(error, wl_ref[...])
         for copy in cnt_copies:
             copy.wait_recv()
         covered = cnt[0]
         for j in range(1, n):
             covered = covered + cnt[j]
         scale = (imitation_weight * pixels) / covered[0:1, 0:1]
-        start = (top_ref[...].astype(f32) + imitation * scale).astype(bf16)
+        error = (mask[:, 0:1] * (lateral - teacher_ref[...].astype(f32)) * scale).astype(bf16)
+        imitation = dot_nt(error, wl_ref[...])
+        start = (top_ref[...].astype(f32) + imitation).astype(bf16)
         start = jnp.where(out_ref[...] > 0, start, jnp.zeros_like(start))
         pas[0] = start[:, :half]
         pas[1] = start[:, half:]
@@ -195,7 +248,7 @@
         q = lo // half
         ps_send[j] = pas[q, :, lo - q * half : lo - q * half + share]
     ps_all[me] = ps_send[me]
-    ps_copies = dp_copies(3, lambda to: ps_send.at[to], ps_all.at[me])
+    ps_copies = dp_copies(3, lambda to: ps_send.at[to, mine], ps_all.at[me, mine])
     for copy in ps_copies:
         copy.start()
 
@@ -209,7 +262,7 @@
             column = None
             for da in (-1, 0, 1):
                 t = 3 * (da + 1) + db + 1
-                y = moved(dot_nt(lhs, taps[t, b * blk : (b + 1) * blk, :]), da, 0)
+                y = moved(dot_nn(lhs, taps[t, b * blk : (b + 1) * blk, :]), da, 0)
                 column = y if column is None else column + y
             column = moved(column, 0, db)
             total = column if total is None else total + column
@@ -219,9 +272,9 @@
 
     dfx_copy = remote(d_all.at[me], dfx, core_send.at[1], core_recv.at[1], {"chan": other})
     dfx_copy.start()
-    d_copies = dp_copies(4, lambda to: d_all.at[me], d_all.at[me])
-    for copy in d_copies:
-        copy.start()
+    moves = [line(step, d_all) for step in range(n - 1)]
+    if moves:
+        line_start(moves[0])
 
     own_rows = pl.ds(pl.multiple_of(c * half, half), half)
     grad = dot_nt(d_first, wr_ref[own_rows, :]) + pas[c].astype(f32)
@@ -256,26 +309,57 @@
         copy.start()
 
     norm = 1.0 / math.sqrt(pixels)
-    for copy in sec_copies + ps_copies:
+    bi_shares = share_copies(0, bi_all)
+    ps_shares = share_copies(1, ps_all)
+    for arrived, on in ((bi_copies, bi_shares), (ps_copies, ps_shares)):
+        for copy, share_copy in zip(arrived, on):
+            copy.wait_recv()
+            share_copy.start()
+    if len(moves) > 1:
+        line_recv(moves[0])
+        line_start(moves[1])
+    ng_copy.wait_recv()
+    stores = []
+    for q in range(2):
+        stores.append(pltpu.make_async_copy(
+            ng.at[q], grads_hbm.at[:, q * half : (q + 1) * half], store_sem.at[q]))
+        stores[q].start()
+    for copy in sec_copies + ps_shares:
         copy.wait_recv()
     expand = dot_tn(sec_all[...].reshape(n * rows, width), ps_all[...].reshape(n * rows, share))
     expand_ref[...] = expand * norm
-    for copy in bi_copies + d_copies:
+    stores.append(pltpu.make_async_copy(expand_ref, expand_hbm, store_sem.at[2]))
+    stores[2].start()
+    for copy in bi_shares:
         copy.wait_recv()
+    for step in range(1, n - 1):
+        line_recv(moves[step])
+        if step + 1 < n - 1:
+            line_start(moves[step + 1])
+    if len(moves) == 1:
+        line_recv(moves[0])
     reduced = dot_tn(bi_all[...].reshape(n * rows, share), d_all[...].reshape(n * rows, width))
     reduce_ref[...] = reduced * norm
+    stores.append(pltpu.make_async_copy(reduce_ref, reduce_hbm, store_sem.at[3]))
+    stores[3].start()
     for copy in g_copies:
         copy.wait_recv()
     g_all[me] = jnp.zeros(g_all.shape[1:], bf16)
     total = gf[me]
     for j in range(n):
         total = total + g_all[j].astype(f32)
-    group_ref[...] = total * norm
-    ng_copy.wait_recv()
-    grads_ref[:, :half] = ng[0]
-    grads_ref[:, half:] = ng[1]
-
-    for copy in cnt_copies + sec_copies + bi_copies + ps_copies + d_copies + g_copies:
+    group_ref[...] = (total * norm)[: 9 * k]
+    stores.append(pltpu.make_async_copy(group_ref, group_hbm, store_sem.at[4]))
+    stores[4].start()
+    for store in stores:
+        store.wait()
+
+    for moved_step in moves:
+        for copy, sends, _ in moved_step:
+            pl.when(sends)(copy.wait_send)
+    for copy in bi_shares + ps_shares:
+        copy.wait_send()
+    for copy in cnt_copies + sec_copies + bi_copies + ps_copies + g_copies:
         copy.wait_send()
     for copy in (wr_copy, dfx_copy, ng_copy):
         copy.wait_send()
@@ -306,10 +390,10 @@
     pixels = rows * n
     share = channels // n
     k = gw // n
-    grows = -(-9 * k // 16) * 16
+    grows = -(-9 * k // 8) * 8
     half = channels // 2
     blk = min(256, width)
-    vmem = pl.BlockSpec(memory_space=pltpu.VMEM)
+    hbm = pl.BlockSpec(memory_space=pl.ANY)
     smem = pl.BlockSpec(memory_space=pltpu.SMEM)
     dma = pltpu.SemaphoreType.DMA
     peers = max(n - 1, 1)
@@ -318,12 +402,26 @@
         out_shape=(
             jax.ShapeDtypeStruct((rows, channels), bf16),
             jax.ShapeDtypeStruct((share, width), f32),
-            jax.ShapeDtypeStruct((grows, width), f32),
+            jax.ShapeDtypeStruct((9 * k, width), f32),
             jax.ShapeDtypeStruct((width, share), f32),
         ),
-        in_specs=[smem, smem] + [vmem] * 10,
-        out_specs=(vmem,) * 4,
+        in_specs=[smem, smem] + [hbm] * 10,
+        out_specs=(hbm,) * 4,
         scratch_shapes=[
+            pltpu.VMEM((rows, channels), bf16),
+            pltpu.VMEM((rows, channels), bf16),
+            pltpu.VMEM((rows, width), bf16),
+            pltpu.VMEM((rows, width), bf16),
+            pltpu.VMEM((channels, width), bf16),
+            pltpu.VMEM((9 * gw * gw, groups), bf16),
+            pltpu.VMEM((width, channels), bf16),
+            pltpu.VMEM((channels, lateral_width), bf16),
+            pltpu.VMEM((rows, lateral_width), bf16),
+            pltpu.VMEM((rows, channels), bf16),
+            pltpu.VMEM((share, width), f32),
+            pltpu.VMEM((9 * k, width), f32),
+            pltpu.VMEM((width, share), f32),
+            dma((10,)), dma((5,)),
             pltpu.VMEM((2, rows, half), bf16),
             pltpu.VMEM((2, rows, half), bf16),
             pltpu.VMEM((half, width), bf16),
@@ -343,18 +441,19 @@
             pltpu.VMEM((9, width // blk, blk, rows), bf16),
             dma((6, peers)), dma((6, peers)), dma((3,)), dma((3,)),
             dma((2,)), dma((2,)), dma((2,)), dma((2,)),
+            dma((peers,)), dma((peers,)), dma((peers,)), dma((peers,)), dma((2, peers)), dma((2, peers)),
         ],
         compiler_params=pltpu.CompilerParams(
             collective_id=0, has_side_effects=True, vmem_limit_bytes=56 << 20,
         ),
     )(
-        boxes.reshape(crops, slots * 4), region_counts.reshape(1, crops),
+        boxes.transpose(0, 2, 1), region_counts.reshape(1, crops),
         block_inputs.reshape(rows, channels), out_pre.reshape(rows, channels),
         first_pre.reshape(rows, width), second_pre.reshape(rows, width),
-        w_reduce[0], w_group.reshape(9 * groups * gw, gw), w_expand[0], w_lateral,
+        w_reduce[0], w_group[0].transpose(0, 2, 3, 1).reshape(9 * gw * gw, groups), w_expand[0], w_lateral,
         teacher.reshape(rows, lateral_width), top_grad.reshape(rows, channels),
     )
-    group = group[: 9 * k].reshape(9, k, groups, gw).transpose(0, 2, 1, 3)
+    group = group.reshape(9, k, groups, gw).transpose(0, 2, 1, 3)
     return (
         grads.reshape(1, crops, side, side, channels), reduced[None], group[None], expand[None],
     )

time: 57 us -> 45.3 us (0.79)
  Pallas kernels: 47.9 us -> 39.6 us
  local copies, waits for them, and re-layouts: 8.31 us -> 4.77 us
    pallas_call x1, Pallas kernels: 47.9 us -> 39.6 us  [on_device(): pl.pallas_call(functools.partial(kernel, (n, sections, crops, side, slots...]
    unnamed x12 -> x10, local copies, waits for them, and re-layouts: 6.49 us -> 3.66 us
    slice x1 -> x0, local copies, waits for them, and re-layouts: 0.96 us -> none  [on_device(): group = group[:9 * k].reshape(9, k, groups, gw).transpose(0, 2, 1, 3)]
where the time goes in v2:
time: 45.3 us; the launch traced here: 45.1 us
  Pallas kernels  39.6 us (87%)
  local copies, waits for them, and re-layouts  4.77 us (11%)
  between operations  0.67 us (1%)
    pallas_call x1, Pallas kernels, on_device(): pl.pallas_call(functools.partial(kernel, (n, sections, crops, side, slots...  39.6 us
    unnamed x10, local copies, waits for them, and re-layouts  3.66 us
    reshape x1, local copies, waits for them, and re-layouts, on_device(): group = group.reshape(9, k, groups, gw).transpose(0, 2, 1, 3)  1.11 us

profile of v2, /device:TPU:0, one launch (start us, length us, event | category | flops | bytes accessed | tf_op | source)
XLA Modules:
  0.0 45.1 jit_solution(16408594574809811582)
XLA Ops:
  0.6 39.6 %shard_map.147 = (bf16[128,1024]{1,0:T(8,128)(2,1)}, f32[256,512]{1,0:T(8,128)}, f32[36,512]{1,0:T(8,128)}, f32[512,256]{1,0:T(8,128)}) custom-call(s32[2,4,8]{2,1,0:T(4,128)} %bitcast.34, s32[1,2]{1,0:T(1,128)} %bitcast.35, bf16[128,1024]{1,0:T(8,128)(2,1)} %bitcast.28, bf16[128,1024]{1,0:T(8,128)(2,1)} %bitcast.29, bf16[128,512]{1,0:T(8,128)(2,1)} %bitcast.31, ...), custom_call_target="tpu_custom_call" | custom-call | tf_op jit(solution)/shard_map/pallas_call | solution.py:400
  40.3 1.1 %reshape.47 = f32[9,4,32,16]{3,2,1,0:T(8,128)S(1)} reshape(f32[36,512]{1,0:T(8,128)} %get-tuple-element.10) | data formatting | bytes 147456 | tf_op jit(solution)/shard_map/reshape | solution.py:456
  41.4 0.0 copy-start.2
  41.4 0.0 copy-start.1
  41.4 0.9 %copy.17 = f32[1,9,32,4,16]{2,4,3,1,0:T(8,128)} copy(f32[1,9,32,4,16]{4,2,3,1,0:T(8,128)S(1)} %bitcast.21) | data formatting | bytes 147456
  42.3 0.0 copy-done.2
  42.4 0.7 %copy.21 = bf16[1,2,8,8,1024]{4,3,2,1,0:T(8,128)(2,1)} copy(bf16[1,2,8,8,1024]{4,3,2,1,0:T(8,128)(2,1)S(1)} %bitcast.27) | data formatting | bytes 524288
  43.1 0.0 copy-done.1
  43.1 0.0 copy-start
  43.1 0.8 %copy.22 = f32[1,256,512]{2,1,0:T(8,128)} copy(f32[1,256,512]{2,1,0:T(8,128)S(1)} %bitcast.26) | data formatting | bytes 1048576
  43.9 0.4 copy-done
  44.3 0.8 %copy.23 = f32[1,512,256]{2,1,0:T(8,128)} copy(f32[1,512,256]{2,1,0:T(8,128)S(1)} %bitcast.25) | data formatting | bytes 1048576
Async XLA Ops:
  41.4 1.0 %copy-start.2 = (bf16[128,1024]{1,0:T(8,128)(2,1)S(1)}, bf16[128,1024]{1,0:T(8,128)(2,1)}, u32[]{:S(2)}) copy-start(bf16[128,1024]{1,0:T(8,128)(2,1)} %get-tuple-element.8) | copy-start | bytes 786436
  41.4 1.6 %copy-start.1 = (f32[256,512]{1,0:T(8,128)S(1)}, f32[256,512]{1,0:T(8,128)}, u32[]{:S(2)}) copy-start(f32[256,512]{1,0:T(8,128)} %get-tuple-element.9) | copy-start | bytes 1572868
  43.1 1.2 %copy-start = (f32[512,256]{1,0:T(8,128)S(1)}, f32[512,256]{1,0:T(8,128)}, u32[]{:S(2)}) copy-start(f32[512,256]{1,0:T(8,128)} %get-tuple-element.11) | copy-start | bytes 1572868

commit v3 on v2

--- a/solution.py
+++ b/solution.py
@@ -80,11 +80,13 @@
                               share_recv.at[which, step - 1], {"chan": other}))
         return out
 
-    def line(step, buf):
-        ahead, behind = buf.at[lax.max(me - step, 0)], buf.at[lax.min(me + step, n - 1)]
-        right = remote(ahead, ahead, right_send.at[step], right_recv.at[step],
+    def line(step, q, buf):
+        part = pl.ds(q * hrows, hrows)
+        ahead = buf.at[lax.max(me - step, 0), part]
+        behind = buf.at[lax.min(me + step, n - 1), part]
+        right = remote(ahead, ahead, right_send.at[step, q], right_recv.at[step, q],
                        {"dp": lax.min(me + 1, n - 1)})
-        left = remote(behind, behind, left_send.at[step], left_recv.at[step],
+        left = remote(behind, behind, left_send.at[step, q], left_recv.at[step, q],
                       {"dp": lax.max(me - 1, 0)})
         return (
             (right, (me - step >= 0) & (me + 1 < n), me - 1 - step >= 0),
@@ -230,8 +232,6 @@
 
     @pl.when(s < last)
     def _():
-        for copy in cnt_copies:
-            copy.wait_recv()
         prepare_first()
         for q in range(2):
             hop_copies[q].wait_recv()
@@ -272,9 +272,10 @@
 
     dfx_copy = remote(d_all.at[me], dfx, core_send.at[1], core_recv.at[1], {"chan": other})
     dfx_copy.start()
-    moves = [line(step, d_all) for step in range(n - 1)]
-    if moves:
-        line_start(moves[0])
+    moves = [[line(step, q, d_all) for q in range(2)] for step in range(n - 1)]
+    for move in moves[:1]:
+        line_start(move[0])
+        line_start(move[1])
 
     own_rows = pl.ds(pl.multiple_of(c * half, half), half)
     grad = dot_nt(d_first, wr_ref[own_rows, :]) + pas[c].astype(f32)
@@ -316,8 +317,9 @@
             copy.wait_recv()
             share_copy.start()
     if len(moves) > 1:
-        line_recv(moves[0])
-        line_start(moves[1])
+        for q in range(2):
+            line_recv(moves[0][q])
+            line_start(moves[1][q])
     ng_copy.wait_recv()
     stores = []
     for q in range(2):
@@ -333,11 +335,13 @@
     for copy in bi_shares:
         copy.wait_recv()
     for step in range(1, n - 1):
-        line_recv(moves[step])
-        if step + 1 < n - 1:
-            line_start(moves[step + 1])
+        for q in range(2):
+            line_recv(moves[step][q])
+            if step + 1 < n - 1:
+                line_start(moves[step + 1][q])
     if len(moves) == 1:
-        line_recv(moves[0])
+        for q in range(2):
+            line_recv(moves[0][q])
     reduced = dot_tn(bi_all[...].reshape(n * rows, share), d_all[...].reshape(n * rows, width))
     reduce_ref[...] = reduced * norm
     stores.append(pltpu.make_async_copy(reduce_ref, reduce_hbm, store_sem.at[3]))
@@ -354,9 +358,15 @@
     for store in stores:
         store.wait()
 
+    @pl.when(s < last)
+    def _():
+        for copy in cnt_copies:
+            copy.wait_recv()
+
     for moved_step in moves:
-        for copy, sends, _ in moved_step:
-            pl.when(sends)(copy.wait_send)
+        for move in moved_step:
+            for copy, sends, _ in move:
+                pl.when(sends)(copy.wait_send)
     for copy in bi_shares + ps_shares:
         copy.wait_send()
     for copy in cnt_copies + sec_copies + bi_copies + ps_copies + g_copies:
@@ -441,7 +451,7 @@
             pltpu.VMEM((9, width // blk, blk, rows), bf16),
             dma((6, peers)), dma((6, peers)), dma((3,)), dma((3,)),
             dma((2,)), dma((2,)), dma((2,)), dma((2,)),
-            dma((peers,)), dma((peers,)), dma((peers,)), dma((peers,)), dma((2, peers)), dma((2, peers)),
+            dma((peers, 2)), dma((peers, 2)), dma((peers, 2)), dma((peers, 2)), dma((2, peers)), dma((2, peers)),
         ],
         compiler_params=pltpu.CompilerParams(
             collective_id=0, has_side_effects=True, vmem_limit_bytes=56 << 20,

time: 45.3 us -> 44.1 us (0.974)
  Pallas kernels: 39.6 us -> 38.4 us
    pallas_call x1, Pallas kernels: 39.6 us -> 38.4 us  [on_device(): pl.pallas_call(functools.partial(kernel, (n, sections, crops, side, slots...]
where the time goes in v3:
time: 44.1 us; the launch traced here: 43.8 us
  Pallas kernels  38.4 us (87%)
  local copies, waits for them, and re-layouts  4.77 us (11%)
  between operations  0.67 us (2%)
    pallas_call x1, Pallas kernels, on_device(): pl.pallas_call(functools.partial(kernel, (n, sections, crops, side, slots...  38.4 us
    unnamed x10, local copies, waits for them, and re-layouts  3.66 us
    reshape x1, local copies, waits for them, and re-layouts, on_device(): group = group.reshape(9, k, groups, gw).transpose(0, 2, 1, 3)  1.11 us

profile of v3, /device:TPU:0, one launch (start us, length us, event | category | flops | bytes accessed | tf_op | source)
XLA Modules:
  0.0 43.8 jit_solution(8245302293213042819)
XLA Ops:
  0.6 38.4 %shard_map.147 = (bf16[128,1024]{1,0:T(8,128)(2,1)}, f32[256,512]{1,0:T(8,128)}, f32[36,512]{1,0:T(8,128)}, f32[512,256]{1,0:T(8,128)}) custom-call(s32[2,4,8]{2,1,0:T(4,128)} %bitcast.34, s32[1,2]{1,0:T(1,128)} %bitcast.35, bf16[128,1024]{1,0:T(8,128)(2,1)} %bitcast.28, bf16[128,1024]{1,0:T(8,128)(2,1)} %bitcast.29, bf16[128,512]{1,0:T(8,128)(2,1)} %bitcast.31, ...), custom_call_target="tpu_custom_call" | custom-call | tf_op jit(solution)/shard_map/pallas_call | solution.py:410
  39.0 1.1 %reshape.47 = f32[9,4,32,16]{3,2,1,0:T(8,128)S(1)} reshape(f32[36,512]{1,0:T(8,128)} %get-tuple-element.10) | data formatting | bytes 147456 | tf_op jit(solution)/shard_map/reshape | solution.py:466
  40.1 0.0 copy-start.2
  40.2 0.0 copy-start.1
  40.2 0.9 %copy.17 = f32[1,9,32,4,16]{2,4,3,1,0:T(8,128)} copy(f32[1,9,32,4,16]{4,2,3,1,0:T(8,128)S(1)} %bitcast.21) | data formatting | bytes 147456
  41.1 0.0 copy-done.2
  41.1 0.7 %copy.21 = bf16[1,2,8,8,1024]{4,3,2,1,0:T(8,128)(2,1)} copy(bf16[1,2,8,8,1024]{4,3,2,1,0:T(8,128)(2,1)S(1)} %bitcast.27) | data formatting | bytes 524288
  41.8 0.0 copy-done.1
  41.8 0.0 copy-start
  41.8 0.8 %copy.22 = f32[1,256,512]{2,1,0:T(8,128)} copy(f32[1,256,512]{2,1,0:T(8,128)S(1)} %bitcast.26) | data formatting | bytes 1048576
  42.6 0.4 copy-done
  43.0 0.8 %copy.23 = f32[1,512,256]{2,1,0:T(8,128)} copy(f32[1,512,256]{2,1,0:T(8,128)S(1)} %bitcast.25) | data formatting | bytes 1048576
Async XLA Ops:
  40.1 1.0 %copy-start.2 = (bf16[128,1024]{1,0:T(8,128)(2,1)S(1)}, bf16[128,1024]{1,0:T(8,128)(2,1)}, u32[]{:S(2)}) copy-start(bf16[128,1024]{1,0:T(8,128)(2,1)} %get-tuple-element.8) | copy-start | bytes 786436
  40.2 1.6 %copy-start.1 = (f32[256,512]{1,0:T(8,128)S(1)}, f32[256,512]{1,0:T(8,128)}, u32[]{:S(2)}) copy-start(f32[256,512]{1,0:T(8,128)} %get-tuple-element.9) | copy-start | bytes 1572868
  41.8 1.2 %copy-start = (f32[512,256]{1,0:T(8,128)S(1)}, f32[512,256]{1,0:T(8,128)}, u32[]{:S(2)}) copy-start(f32[512,256]{1,0:T(8,128)} %get-tuple-element.11) | copy-start | bytes 1572868
